TPU v7x, 32 devices: a whole 2x2x4 slice. The times are simulated.
32 devices in a mesh: ctx: 8 (over z, x), tp: 4 (over y, core).
Axes of the slice: x: 2, y: 2, z: 4, core: 2. Of those that a mesh axis runs over, the one named last changes fastest.
Arguments:
- inputs: bfloat16 [4096, 768], P(('ctx', 'tp')), may hold values from -6 to 6
- positions: int32 [4096], P('ctx'), may hold values from 0 to 3071, as said below
- attn_scale: float32 [768], replicated, may hold values from 0.1 to 1.9
- attn_shift: float32 [768], replicated, may hold values from -4 to 4
- mlp_scale: float32 [768], replicated, may hold values from 0.1 to 1.9
- mlp_shift: float32 [768], replicated, may hold values from -4 to 4
- qkv_weight: bfloat16 [768, 3, 768], P(None, None, 'tp'), may hold values from -0.21875 to 0.21875
- qv_bias: float32 [2, 768], P(None, 'tp'), may hold values from -4 to 4
- dense_weight: bfloat16 [768, 768], P('tp'), may hold values from -1.75 to 1.75
- dense_bias: float32 [768], replicated, may hold values from -5 to 5
- up_weight: bfloat16 [768, 3072], P(None, 'tp'), may hold values from -0.21875 to 0.21875
- up_bias: float32 [3072], P('tp'), may hold values from -4 to 4
- down_weight: bfloat16 [3072, 768], P('tp'), may hold values from -0.109375 to 0.109375
- down_bias: float32 [768], replicated, may hold values from -5 to 5
- cotangent: bfloat16 [4096, 768], P(('ctx', 'tp')), may hold values from -6 to 6
Outputs:
- output: bfloat16 [4096, 768], P(('ctx', 'tp'))
- grad_input: float32 [4096, 768], P(('ctx', 'tp'))
- grad_attn_scale: float32 [768], replicated
- grad_attn_shift: float32 [768], replicated
- grad_mlp_scale: float32 [768], replicated
- grad_mlp_shift: float32 [768], replicated
- grad_qkv: float32 [768, 3, 768], P(None, None, 'tp')
- grad_qv_bias: float32 [2, 768], P(None, 'tp')
- grad_dense: float32 [768, 768], P('tp')
- grad_dense_bias: float32 [768], replicated
- grad_up: float32 [768, 3072], P(None, 'tp')
- grad_up_bias: float32 [3072], P('tp')
- grad_down: float32 [3072, 768], P('tp')
- grad_down_bias: float32 [768], replicated
Inputs may be any that keep to these rules, and one draw needn't show every extreme that they name: The sequence holds three documents; positions count from 0 at each document's first token and rise by one along it; the second document has 3072 tokens and starts at a token between 1 and 1023.
All inputs are finite; a program needn't handle non-finite values.
Results may differ from a plain program's by a relative error of at most 0.025.
Values may be sent and summed in bfloat16 or wider, within the bound.
A program may use at most 128 MiB of HBM per device.

v0:
```python
import math

import jax
import jax.numpy as jnp
from jax import lax
from jax.sharding import PartitionSpec as P

D = 768
HD = 64
ROT = 16


norm_eps = 1e-05


def layer_norm(values, scale, shift):
    mean_value = jnp.mean(values, axis=-1, keepdims=True)
    centred = values - mean_value
    variance = jnp.mean(centred * centred, axis=-1, keepdims=True)
    inv_std = lax.rsqrt(variance + norm_eps)
    normal_part = centred * inv_std
    return (normal_part * scale + shift, normal_part, inv_std)


def norm_backward(grad_normed, normal_part, inv_std, scale):
    grad_hat = grad_normed * scale
    mean_grad = jnp.mean(grad_hat, axis=-1, keepdims=True)
    mean_mixed = jnp.mean(grad_hat * normal_part, axis=-1, keepdims=True)
    return inv_std * (grad_hat - mean_grad - normal_part * mean_mixed)


def rotary_tables(positions):
    freqs = 10000.0 ** (-jnp.arange(0, ROT, 2).astype(jnp.float32) / ROT)
    angles = positions.astype(jnp.float32)[:, None] * freqs[None, :]
    angles = jnp.concatenate([angles, angles], axis=1)
    return (jnp.cos(angles), jnp.sin(angles))


def rotate(tensor, cosines, sines):
    part = tensor[..., :ROT]
    half = ROT // 2
    turned = jnp.concatenate([-part[..., half:], part[..., :half]], axis=-1)
    spun = part * cosines[:, None, :] + turned * sines[:, None, :]
    return jnp.concatenate([spun, tensor[..., ROT:]], axis=-1)


def gelu_grad(pre_act):
    cumulative = 0.5 * (1.0 + jax.scipy.special.erf(pre_act * 0.7071067811865476))
    density = jnp.exp(-0.5 * pre_act * pre_act) * 0.3989422804014327
    return cumulative + pre_act * density


def block_length(length):
    return math.gcd(length, 1024)


def local(
    inputs,
    positions,
    attn_scale,
    attn_shift,
    mlp_scale,
    mlp_shift,
    qkv_weight,
    qv_bias,
    dense_weight,
    dense_bias,
    up_weight,
    up_bias,
    down_weight,
    down_bias,
    cotangent,
):
    local_width = qkv_weight.shape[2]
    head_count = local_width // HD
    score_scale = HD ** (-0.5)
    resid = inputs.astype(jnp.float32)
    normed_one, hat_one, std_one = layer_norm(resid, attn_scale, attn_shift)
    normed_two, hat_two, std_two = layer_norm(resid, mlp_scale, mlp_shift)
    attn_in, mlp_in = (
        lax.all_gather(normed_one.astype(jnp.bfloat16), "tp", axis=0, tiled=True),
        lax.all_gather(normed_two.astype(jnp.bfloat16), "tp", axis=0, tiled=True),
    )
    block_rows = attn_in.shape[0]
    proj = jnp.dot(
        attn_in, qkv_weight.reshape(D, 3 * local_width), preferred_element_type=jnp.float32
    )
    proj = proj.reshape(block_rows, 3, head_count, HD)
    cosines, sines = rotary_tables(positions)
    queries = rotate(proj[:, 0] + qv_bias[0].reshape(head_count, HD), cosines, sines).astype(
        jnp.bfloat16
    )
    keys_rot = rotate(proj[:, 1], cosines, sines).astype(jnp.bfloat16)
    values = (proj[:, 2] + qv_bias[1].reshape(head_count, HD)).astype(jnp.bfloat16)
    own_start = lax.axis_index("ctx") * block_rows
    query_pos = own_start + jnp.arange(block_rows, dtype=jnp.int32)
    first_key = query_pos - positions
    last_query = query_pos[block_rows - 1]
    earliest_key = jnp.min(first_key)

    def visible_mask(start_row, length):
        key_pos = start_row + jnp.arange(length, dtype=jnp.int32)
        return (key_pos[None, :] <= query_pos[:, None]) & (key_pos[None, :] >= first_key[:, None])

    def reachable(start_row, length):
        return (start_row <= last_query) & (start_row + length - 1 >= earliest_key)

    def attend_block(running, key_block, value_block, start_row):
        row_max, row_sum, accumulated = running
        visible = visible_mask(start_row, key_block.shape[0])
        scores = (
            jnp.einsum("qhd,khd->hqk", queries, key_block, preferred_element_type=jnp.float32)
            * score_scale
        )
        scores = jnp.where(visible[None], scores, -1e30)
        new_max = jnp.maximum(row_max, jnp.max(scores, axis=-1))
        weights = jnp.where(visible[None], jnp.exp(scores - new_max[..., None]), 0.0)
        factor = jnp.exp(row_max - new_max)
        row_sum = row_sum * factor + jnp.sum(weights, axis=-1)
        accumulated = accumulated * factor[..., None] + jnp.einsum(
            "hqk,khd->hqd",
            weights.astype(jnp.bfloat16),
            value_block,
            preferred_element_type=jnp.float32,
        )
        return (new_max, row_sum, accumulated)

    initial = (
        jnp.full((head_count, block_rows), -1e30, jnp.float32),
        jnp.zeros((head_count, block_rows), jnp.float32),
        jnp.zeros((head_count, block_rows, HD), jnp.float32),
    )
    running = initial
    key_rows = lax.all_gather(keys_rot, "ctx", axis=0, tiled=True)
    value_rows = lax.all_gather(values, "ctx", axis=0, tiled=True)
    length = key_rows.shape[0]
    attend_step_rows = block_length(length)
    steps_count = length // attend_step_rows
    key_blocks = key_rows.reshape(steps_count, attend_step_rows, head_count, HD)
    value_blocks = value_rows.reshape(steps_count, attend_step_rows, head_count, HD)

    def one_step(current, inputs_step):
        key_block, value_block, number = inputs_step
        block_start = number * attend_step_rows

        def attend_now(state):
            return attend_block(state, key_block, value_block, block_start)

        def keep_state(state):
            return state

        return (
            lax.cond(reachable(block_start, attend_step_rows), attend_now, keep_state, current),
            None,
        )

    running, unused = lax.scan(
        one_step, running, (key_blocks, value_blocks, jnp.arange(steps_count, dtype=jnp.int32))
    )
    row_max, row_sum, accumulated = running
    attended = jnp.transpose(accumulated / row_sum[..., None], (1, 0, 2)).astype(jnp.bfloat16)
    log_total = row_max + jnp.log(row_sum)
    attended_flat = attended.reshape(block_rows, local_width)
    attn_part = jnp.dot(attended_flat, dense_weight, preferred_element_type=jnp.float32)
    pre_act = jnp.dot(mlp_in, up_weight, preferred_element_type=jnp.float32) + up_bias
    activation = jax.nn.gelu(pre_act, approximate=False).astype(jnp.bfloat16)
    mlp_part = jnp.dot(activation, down_weight, preferred_element_type=jnp.float32)
    branch_sum = lax.psum_scatter(attn_part + mlp_part, "tp", scatter_dimension=0, tiled=True)
    output = (resid + branch_sum + dense_bias + down_bias).astype(jnp.bfloat16)
    grad_out = cotangent.astype(jnp.float32)
    bias_grad = jnp.sum(grad_out, axis=0)
    grad_full = lax.all_gather(cotangent, "tp", axis=0, tiled=True)
    grad_down = jnp.dot(activation.T, grad_full, preferred_element_type=jnp.float32)
    grad_act = jnp.dot(grad_full, down_weight.T, preferred_element_type=jnp.float32)
    grad_pre = grad_act * gelu_grad(pre_act)
    grad_up_bias = jnp.sum(grad_pre, axis=0)
    grad_pre_low = grad_pre.astype(jnp.bfloat16)
    grad_up = jnp.dot(mlp_in.T, grad_pre_low, preferred_element_type=jnp.float32)
    grad_mlp_in = jnp.dot(grad_pre_low, up_weight.T, preferred_element_type=jnp.float32)
    grad_dense = jnp.dot(attended_flat.T, grad_full, preferred_element_type=jnp.float32)
    grad_attended = jnp.dot(grad_full, dense_weight.T, preferred_element_type=jnp.float32)
    grad_attended = grad_attended.astype(jnp.bfloat16).reshape(block_rows, head_count, HD)
    delta_rows = jnp.transpose(
        jnp.sum(grad_attended.astype(jnp.float32) * attended.astype(jnp.float32), axis=-1)
    )

    def score_grads(query_rows, grad_rows, log_rows, delta_part, key_block, value_block, visible):
        scores = (
            jnp.einsum("qhd,khd->hqk", query_rows, key_block, preferred_element_type=jnp.float32)
            * score_scale
        )
        weights = jnp.where(visible[None], jnp.exp(scores - log_rows[..., None]), 0.0)
        grad_weights = jnp.einsum(
            "qhd,khd->hqk", grad_rows, value_block, preferred_element_type=jnp.float32
        )
        grad_scores = (weights * (grad_weights - delta_part[..., None])).astype(jnp.bfloat16)
        return (weights.astype(jnp.bfloat16), grad_scores)

    key_back, value_back = (
        lax.all_gather(keys_rot, "ctx", axis=0, tiled=True),
        lax.all_gather(values, "ctx", axis=0, tiled=True),
    )
    total_rows = key_back.shape[0]
    step_rows = block_length(total_rows)
    steps_count = total_rows // step_rows
    back_inputs = (
        key_back.reshape(steps_count, step_rows, head_count, HD),
        value_back.reshape(steps_count, step_rows, head_count, HD),
        jnp.arange(steps_count, dtype=jnp.int32),
    )
    zero_query = jnp.zeros((block_rows, head_count, HD), jnp.float32)

    def back_step(query_grad, inputs_step):
        key_block, value_block, number = inputs_step
        block_start = number * step_rows

        def with_terms(grad_now):
            visible = visible_mask(block_start, step_rows)
            weights_low, grad_scores = score_grads(
                queries, grad_attended, log_total, delta_rows, key_block, value_block, visible
            )
            grad_now = (
                grad_now
                + jnp.einsum(
                    "hqk,khd->qhd", grad_scores, key_block, preferred_element_type=jnp.float32
                )
                * score_scale
            )
            key_part = (
                jnp.einsum("hqk,qhd->khd", grad_scores, queries, preferred_element_type=jnp.float32)
                * score_scale
            )
            value_part = jnp.einsum(
                "hqk,qhd->khd", weights_low, grad_attended, preferred_element_type=jnp.float32
            )
            joined = jnp.concatenate(
                [
                    key_part.reshape(step_rows, local_width),
                    value_part.reshape(step_rows, local_width),
                ],
                axis=1,
            )
            return (grad_now, joined)

        def without_terms(grad_now):
            return (grad_now, jnp.zeros((step_rows, 2 * local_width), jnp.float32))

        return lax.cond(reachable(block_start, step_rows), with_terms, without_terms, query_grad)

    query_grad, key_terms = lax.scan(back_step, zero_query, back_inputs)
    key_terms = key_terms.reshape(total_rows, 2 * local_width)
    own_terms = lax.psum_scatter(key_terms, "ctx", scatter_dimension=0, tiled=True)
    key_grad = own_terms[:, :local_width].reshape(block_rows, head_count, HD)
    value_grad = own_terms[:, local_width:].reshape(block_rows, head_count, HD)
    grad_query_pre = rotate(query_grad, cosines, -sines)
    grad_key_pre = rotate(key_grad, cosines, -sines)
    qv_bias_grad = jnp.stack(
        [
            jnp.sum(grad_query_pre, axis=0).reshape(local_width),
            jnp.sum(value_grad, axis=0).reshape(local_width),
        ]
    )
    grad_proj = jnp.stack([grad_query_pre, grad_key_pre, value_grad], axis=1)
    grad_proj = grad_proj.reshape(block_rows, 3 * local_width).astype(jnp.bfloat16)
    grad_qkv = jnp.dot(attn_in.T, grad_proj, preferred_element_type=jnp.float32).reshape(
        D, 3, local_width
    )
    grad_attn_in = jnp.dot(
        grad_proj, qkv_weight.reshape(D, 3 * local_width).T, preferred_element_type=jnp.float32
    )
    own_attn, own_mlp = (
        lax.psum_scatter(grad_attn_in, "tp", scatter_dimension=0, tiled=True),
        lax.psum_scatter(grad_mlp_in, "tp", scatter_dimension=0, tiled=True),
    )
    grad_input = grad_out + norm_backward(own_attn, hat_one, std_one, attn_scale)
    grad_input = grad_input + norm_backward(own_mlp, hat_two, std_two, mlp_scale)
    norm_sums = lax.psum(
        (
            jnp.sum(own_attn * hat_one, axis=0),
            jnp.sum(own_attn, axis=0),
            jnp.sum(own_mlp * hat_two, axis=0),
            jnp.sum(own_mlp, axis=0),
            bias_grad,
        ),
        ("ctx", "tp"),
    )
    weight_sums = lax.psum(
        (grad_qkv, qv_bias_grad, grad_dense, grad_up, grad_up_bias, grad_down), "ctx"
    )
    return (
        output,
        grad_input,
        norm_sums[0],
        norm_sums[1],
        norm_sums[2],
        norm_sums[3],
        weight_sums[0],
        weight_sums[1],
        weight_sums[2],
        norm_sums[4],
        weight_sums[3],
        weight_sums[4],
        weight_sums[5],
        norm_sums[4],
    )


def solution(mesh):
    in_specs = (
        P(("ctx", "tp"), None),
        P("ctx"),
        P(),
        P(),
        P(),
        P(),
        P(None, None, "tp"),
        P(None, "tp"),
        P("tp", None),
        P(),
        P(None, "tp"),
        P("tp"),
        P("tp", None),
        P(),
        P(("ctx", "tp"), None),
    )
    out_specs = (
        P(("ctx", "tp"), None),
        P(("ctx", "tp"), None),
        P(),
        P(),
        P(),
        P(),
        P(None, None, "tp"),
        P(None, "tp"),
        P("tp", None),
        P(),
        P(None, "tp"),
        P("tp"),
        P("tp", None),
        P(),
    )
    return jax.shard_map(local, mesh=mesh, in_specs=in_specs, out_specs=out_specs, check_vma=False)
```

profile of v0, /device:TPU:0, one launch (start us, length us, event | category | flops | bytes accessed | tf_op | source)
XLA Modules:
  0.0 690.6 jit_solution(9488253124478135631)
XLA Ops:
  9.6 1.9 fusion.74
  11.5 10.1 %all_gather.17 = bf16[512,768]{1,0:T(8,128)(2,1)S(1)} all-gather(bf16[128,768]{1,0:T(8,128)(2,1)S(1)} %get-tuple-element.958), channel_id=1, replica_groups=mesh['ctx'=8,'tp'=4] {'tp'}, dimensions={0}, use_global_device_ids=true | all-gather | bytes 983040 | tf_op jit(solution)/shard_map/all_gather | solution.py:81
  27.7 8.7 %all_gather.21 = bf16[512,768]{1,0:T(8,128)(2,1)S(1)} all-gather(bf16[128,768]{1,0:T(8,128)(2,1)S(1)} %copy-done.29), channel_id=1, replica_groups=mesh['ctx'=8,'tp'=4] {'tp'}, dimensions={0}, use_global_device_ids=true | all-gather | bytes 983040 | tf_op jit(solution)/shard_map/all_gather | solution.py:172
  37.7 33.9 %all-gather.3.cloned.1.call-done = bf16[4096,3,64]{0,2,1:T(8,128)(2,1)} async-done(((bf16[512,3,64]{0,2,1:T(8,128)(2,1)}), bf16[4096,3,64]{0,2,1:T(8,128)(2,1)}) %all-gather.3.cloned.1.call-update) | async-done | bytes 1572880 | tf_op jit(solution)/shard_map/all_gather | solution.py:134
  71.6 1.6 copy.75
  73.2 43.7 %all-gather.5.cloned.1.call-done = bf16[4096,3,64]{0,2,1:T(8,128)(2,1)} async-done(((bf16[512,3,64]{0,2,1:T(8,128)(2,1)}), bf16[4096,3,64]{0,2,1:T(8,128)(2,1)}) %all-gather.5.cloned.1.call-update) | async-done | bytes 1572880 | tf_op jit(solution)/shard_map/all_gather | solution.py:135
  116.9 2.7 copy.74
  120.1 23.0 %while.39 = (s32[]{:T(128)}, f32[3,512]{1,0:T(4,128)S(1)}, f32[3,512]{1,0:T(4,128)S(1)}, f32[3,512,64]{1,2,0:T(8,128)S(1)}, s32[4]{0:T(128)}, /*index=5*/s32[]{:...) while((s32[]{:T(128)}, f32[3,512]{1,0:T(4,128)S(1)}, ...), condition=%wide.region_8.9_spmd.clone, body=%wide.region_3.8_spmd.clone.sunk | while | flops 424874496 | bytes 22858608 | solution.py:157
  120.1 1.2 dynamic_slice.82
  123.9 7.8 %conditional.6 = ((f32[3,512]{1,0:T(4,128)S(1)}, f32[3,512]{1,0:T(4,128)S(1)}, f32[3,512,64]{1,2,0:T(8,128)S(1)})) conditional(s32[]{:T(128)} %convert_element_type.207, (f32[3,512]{1,0:T(4,128)S(1)}, f32[3,512]{1,0:T(4,128)S(1)}, f32[3,512,64]{1,2,0:T(8,128)S(1)}) %tuple.156, (s32[]{:T(128)}, s32[]{:T(128)}, s32[512]{0:T(512)}, ...), branch_computations={%region_4.4_spmd, %region_5.7_spmd} | conditional | flops 424874496 | bytes 22856236 | solution.py:153
  125.8 1.4 fusion.4
  127.2 1.6 fusion.6
  128.8 3.0 fusion.10
  143.7 1.4 multiply_reduce_fusion
  145.1 37.2 %while.40 = (s32[]{:T(128)}, f32[512,3,64]{0,2,1:T(8,128)S(1)}, f32[4,1024,384]{2,1,0:T(8,128)}, s32[4]{0:T(128)S(1)}, s32[]{:T(128)}, /*index=5*/s32[]{:T(128)}...) while((s32[]{:T(128)}, f32[512,3,64]{0,2,1:T(8,128)S(1)}, ...), condition=%wide.region_14.15_spmd.clone, body=%wide.region_11.14_spmd.clone.sunk | while | flops 1024722432 | bytes 56325616 | solution.py:250
  147.8 8.3 %conditional.7 = (f32[512,3,64]{0,2,1:T(8,128)S(1)}, f32[1,1024,384]{1,2,0:T(8,128)S(1)}) conditional(s32[]{:T(128)} %convert_element_type.208, f32[512,3,64]{0,2,1:T(8,128)S(1)} %get-tuple-element.1217, (s32[]{:T(128)}, s32[]{:T(128)}, s32[512]{0:T(512)}, bf16[4,1024,3,64]{1,3,2,0:T(8,128)(2,1)S(1)}, s32[]{:T(128)}, ...), branch_computations={%region_12.12_spmd, %region_13.13_spmd} | conditional | flops 1024722432 | bytes 37448308 | solution.py:248
  149.4 3.3 fusion.23
  153.4 1.5 fusion.25
  156.1 1.6 copy.77
  157.7 2.8 constant_dynamic-update-slice_fusion.2
  163.4 1.6 copy.77
  165.0 2.8 constant_dynamic-update-slice_fusion.2
  170.6 1.6 copy.77
  172.3 2.8 constant_dynamic-update-slice_fusion.2
  177.9 1.6 copy.77
  179.5 2.8 constant_dynamic-update-slice_fusion.2
  183.3 8.7 %all_gather.20 = bf16[512,768]{1,0:T(8,128)(2,1)S(1)} all-gather(bf16[128,768]{1,0:T(8,128)(2,1)S(1)} %copy-done.31), channel_id=1, replica_groups=mesh['ctx'=8,'tp'=4] {'tp'}, dimensions={0}, use_global_device_ids=true | all-gather | bytes 983040 | tf_op jit(solution)/shard_map/all_gather | solution.py:82
  192.0 4.2 fusion.44
  198.3 2.0 fusion.93
  201.8 144.9 %reduce-scatter.7.cloned.1.call-done = f32[512,384]{1,0:T(8,128)} async-done(((f32[4096,384]{1,0:T(8,128)}), f32[512,384]{1,0:T(8,128)}) %reduce-scatter.7.cloned.1.call-update) | async-done | bytes 786448 | tf_op jit(solution)/shard_map/reduce_scatter | solution.py:252
  346.7 2.0 slice.122
  348.6 1.8 copy.47
  351.4 1.3 copy.46
  354.5 2.0 fusion.111
  357.9 2.0 convolution_add_fusion
  361.0 3.3 fusion.91
  364.4 2.2 fusion.113
  368.1 1.8 fusion.59
  371.1 20.6 %all-reduce.1 = (f32[2,192]{1,0:T(2,128)}, f32[768]{0:T(1024)}) all-reduce(f32[2,192]{1,0:T(2,128)S(1)} %pad_maximum_fusion.4, f32[768]{0:T(1024)S(1)} %get-tuple-element.970), channel_id=1, replica_groups=mesh['ctx'=8,'tp'=4] {'ctx'}, use_global_device_ids=true, to_apply=%region_33.34 | all-reduce | flops 1152 | bytes 9216 | tf_op jit(solution)/shard_map/psum | solution.py:287
  391.7 15.1 %reduce-scatter.9.cloned.1.call-done = f32[128,768]{1,0:T(8,128)} async-done(((f32[512,768]{1,0:T(8,128)}), f32[128,768]{1,0:T(8,128)}) %reduce-scatter.9.cloned.1.call-update) | async-done | bytes 393232 | tf_op jit(solution)/shard_map/reduce_scatter | solution.py:272
  406.8 1.5 fusion.82
  408.3 28.9 %reduce-scatter.5.cloned.1.call-done = f32[128,768]{1,0:T(8,128)} async-done(((f32[512,768]{1,0:T(8,128)}), f32[128,768]{1,0:T(8,128)}) %reduce-scatter.5.cloned.1.call-update) | async-done | bytes 393232 | tf_op jit(solution)/shard_map/reduce_scatter | solution.py:168
  437.2 2.3 convert_reduce_fusion.1
  439.5 43.0 %all-reduce = (f32[768]{0:T(1024)}, f32[768]{0:T(1024)}, f32[768]{0:T(1024)}, f32[768]{0:T(1024)}, f32[768]{0:T(1024)S(1)}) all-reduce(f32[768]{0:T(1024)S(1)} %get-tuple-element.862, f32[768]{0:T(1024)S(1)} %get-tuple-element.867, f32[768]{0:T(1024)S(1)} %get-tuple-element.871, ...), channel_id=1, replica_groups=mesh['ctx'=8,'tp'=4] {'ctx','tp'}, use_global_device_ids=true, to_apply=%region_23.24 | all-reduce | flops 3840 | bytes 30720 | tf_op jit(solution)/shard_map/psum | solution.py:277
  482.5 192.9 %all-reduce.5.cloned.1.call-done = (f32[768,3,192]{0,2,1:T(8,128)}, f32[192,768]{1,0:T(8,128)}, f32[768,768]{1,0:T(8,128)}, f32[768,768]{1,0:T(8,128)}) async-done(((f32[768,3,192]{0,2,1:T(8,128)}, f32[192,768]{1,0:T(8,128)}, f32[768,768]{1,0:T(8,128)}, f32[768,768]{1,0:T(8,128)}), (f32[768,3,192]{0,2,1:T(8,128)}, f32[192,768]{1,0:T(8,128)}, f32[768,768]{1,0:T(8,128)}, ...) | async-done | bytes 7077904 | tf_op jit(solution)/shard_map/psum | solution.py:287
  676.0 2.9 copy.118
  679.8 1.4 copy.120
  682.3 1.4 copy.121
  (221 shorter events, 40.8 us)
Async XLA Ops:
  7.2 184.8 %copy-start = (bf16[768,768]{1,0:T(8,128)(2,1)S(1)}, bf16[768,768]{1,0:T(8,128)(2,1)}, u32[]{:S(2)}) copy-start(bf16[768,768]{1,0:T(8,128)(2,1)} %param.33) | copy-start | bytes 3538948
  7.2 14.4 %copy-start.12 = (bf16[768,3,192]{0,2,1:T(8,128)(2,1)S(1)}, bf16[768,3,192]{0,2,1:T(8,128)(2,1)}, u32[]{:S(2)}) copy-start(bf16[768,3,192]{0,2,1:T(8,128)(2,1)} %param.29) | copy-start | bytes 2654212
  7.2 64.4 %all-gather.3.cloned.1.call-start = ((), (), s32[]{:S(2)}) async-start(), calls=%async_computation.4 | async-start | bytes 1769472 | tf_op jit(solution)/shard_map/all_gather | solution.py:134
  8.5 13.1 %copy-start.41 = (f32[128]{0:T(128)}, f32[128]{0:T(128)S(1)}, u32[]{:S(2)}) copy-start(f32[128]{0:T(128)S(1)} %broadcast_multiply_fusion.5) | copy-start | bytes 1540
  9.6 12.0 %copy-start.44 = (f32[128]{0:T(128)}, f32[128]{0:T(128)S(1)}, u32[]{:S(2)}) copy-start(f32[128]{0:T(128)S(1)} %add_rsqrt_fusion) | copy-start | bytes 1540
  23.5 4.2 copy-start.29
  24.8 12.5 %copy-start.23 = (bf16[192,768]{1,0:T(8,128)(2,1)S(1)}, bf16[192,768]{1,0:T(8,128)(2,1)}, u32[]{:S(2)}) copy-start(bf16[192,768]{1,0:T(8,128)(2,1)} %param.31) | copy-start | bytes 884740
  25.5 12.2 %copy-start.34 = (f32[512,16]{0,1:T(8,128)}, f32[512,16]{0,1:T(8,128)S(1)}, u32[]{:S(2)}) copy-start(f32[512,16]{0,1:T(8,128)S(1)} %get-tuple-element.966) | copy-start | bytes 98308
  26.2 90.6 %all-gather.5.cloned.1.call-start = ((), (), s32[]{:S(2)}) async-start(), calls=%async_computation.5 | async-start | bytes 1769472 | tf_op jit(solution)/shard_map/all_gather | solution.py:135
  27.0 319.7 %reduce-scatter.7.cloned.1.call-start = ((), (), s32[]{:S(2)}) async-start(), calls=%async_computation.7 | async-start | bytes 7077888 | tf_op jit(solution)/shard_map/reduce_scatter | solution.py:252
  145.1 2.7 copy-start.1
  147.8 1.6 copy-start.40
  147.8 1.6 copy-start.43
  157.7 2.8 copy-start.2
  160.5 2.6 copy-start.1
  165.0 2.8 copy-start.2
  167.8 2.6 copy-start.1
  172.2 2.8 copy-start.2
  175.0 2.6 copy-start.1
  179.5 2.8 copy-start.2
  182.3 9.7 %copy-start.51 = (f32[768]{0:T(1024)S(1)}, f32[768]{0:T(1024)}, u32[]{:S(2)}) copy-start(f32[768]{0:T(1024)} %param.34) | copy-start | bytes 9220
  182.4 209.3 %reduce-scatter.11.cloned.1.call-start = ((), (), s32[]{:S(2)}) async-start(), calls=%async_computation.9 | async-start | bytes 1966080 | tf_op jit(solution)/shard_map/reduce_scatter | solution.py:273
  192.0 4.3 copy-start.7
  192.0 4.3 copy-start.4
  192.0 4.3 copy-start.21
  200.3 206.5 %reduce-scatter.9.cloned.1.call-start = ((), (), s32[]{:S(2)}) async-start(), calls=%async_computation.8 | async-start | bytes 1966080 | tf_op jit(solution)/shard_map/reduce_scatter | solution.py:272
  346.7 3.7 copy-start.18
  351.3 2.2 copy-start.27
  351.3 2.3 copy-start.28
  352.6 1.9 copy-start.13
  354.5 2.1 copy-start.19
  354.5 2.1 copy-start.24
  356.5 80.6 %reduce-scatter.5.cloned.1.call-start = ((), (), s32[]{:S(2)}) async-start(), calls=%async_computation.6 | async-start | bytes 1966080 | tf_op jit(solution)/shard_map/reduce_scatter | solution.py:168
  359.9 315.5 %all-reduce.5.cloned.1.call-start = ((), (), s32[]{:S(2)}) async-start(), calls=%async_computation.10 | async-start | bytes 14155776 | tf_op jit(solution)/shard_map/psum | solution.py:287
  364.4 2.2 copy-start.20
  366.6 1.5 copy-start.10
  369.9 36.9 %copy-start.11 = (bf16[128,768]{1,0:T(8,128)(2,1)S(1)}, bf16[128,768]{1,0:T(8,128)(2,1)}, u32[]{:S(2)}) copy-start(bf16[128,768]{1,0:T(8,128)(2,1)} %param.23) | copy-start | bytes 589828
  369.9 36.9 %copy-start.38 = (f32[768]{0:T(1024)S(1)}, f32[768]{0:T(1024)}, u32[]{:S(2)}) copy-start(f32[768]{0:T(1024)} %param.27) | copy-start | bytes 9220
  369.9 36.9 %copy-start.39 = (f32[768]{0:T(1024)S(1)}, f32[768]{0:T(1024)}, u32[]{:S(2)}) copy-start(f32[768]{0:T(1024)} %param.25) | copy-start | bytes 9220
  369.9 36.8 %copy-start.42 = (f32[128]{0:T(128)S(1)}, f32[128]{0:T(128)}, u32[]{:S(2)}) copy-start(f32[128]{0:T(128)} %copy-done.41) | copy-start | bytes 1540
  369.9 36.8 %copy-start.45 = (f32[128]{0:T(128)S(1)}, f32[128]{0:T(128)}, u32[]{:S(2)}) copy-start(f32[128]{0:T(128)} %copy-done.44) | copy-start | bytes 1540
  369.9 67.2 %copy-start.46 = (f32[768]{0:T(1024)S(1)}, f32[768]{0:T(1024)}, u32[]{:S(2)}) copy-start(f32[768]{0:T(1024)} %param.36) | copy-start | bytes 9220
  369.9 67.2 %copy-start.47 = (f32[768]{0:T(1024)S(1)}, f32[768]{0:T(1024)}, u32[]{:S(2)}) copy-start(f32[768]{0:T(1024)} %param.32) | copy-start | bytes 9220
  370.9 66.3 %copy-start.30 = (bf16[128,768]{1,0:T(8,128)(2,1)S(1)}, bf16[128,768]{1,0:T(8,128)(2,1)}, u32[]{:S(2)}) copy-start(bf16[128,768]{1,0:T(8,128)(2,1)} %param.37) | copy-start | bytes 589828
  482.5 196.5 %copy-start.48 = (f32[768]{0:T(1024)}, f32[768]{0:T(1024)S(1)}, u32[]{:S(2)}) copy-start(f32[768]{0:T(1024)S(1)} %get-tuple-element.1287) | copy-start | bytes 9220
  676.0 3.0 copy-start.33
  676.0 3.8 copy-start.17
  679.8 2.5 copy-start.16
  (17 other events, 16.2 us)
Sparse Core Ops, SparseCore 0:
  26.3 45.2 all-gather.2
  74.2 42.5 all-gather.4
  182.5 164.1 reduce-scatter.6
  349.1 27.2 reduce-scatter.10
  378.7 27.9 reduce-scatter.8
  409.1 27.9 reduce-scatter.4
  442.7 232.6 all-reduce.4
where the time goes:
time: 692 us; the launch traced here: 691 us
  waiting for transfers between devices  460 us (66%)
  blocking collectives  91.2 us (13%)
  local copies, waits for them, and re-layouts  54.8 us (8%)
  matrix products  33.3 us (5%)
  other arithmetic  20.3 us (3%)
  loops' own time  16 us (2%)
  between operations  14.7 us (2%)
    psum x1, waiting for transfers between devices, local(): lax.psum((grad_qkv, qv_bias_grad, grad_dense, grad_up, grad_up_bias, grad...  193 us
    reduce_scatter x1, waiting for transfers between devices, local(): lax.psum_scatter(key_terms, 'ctx', scatter_dimension=0, tiled=True)  145 us
    all_gather x1, waiting for transfers between devices, local(): value_rows = lax.all_gather(values, 'ctx', axis=0, tiled=True)  43.7 us
    psum x1, blocking collectives, local(): lax.psum((jnp.sum(own_attn * hat_one, axis=0), jnp.sum(own_attn, axis=0),...  43 us
    all_gather x1, waiting for transfers between devices, local(): key_rows = lax.all_gather(keys_rot, 'ctx', axis=0, tiled=True)  33.9 us
    reduce_scatter x1, waiting for transfers between devices, local(): lax.psum_scatter(attn_part + mlp_part, 'tp', scatter_dimension=0, tiled=T...  28.9 us
    psum x1, blocking collectives, local(): lax.psum((grad_qkv, qv_bias_grad, grad_dense, grad_up, grad_up_bias, grad...  20.6 us
    dynamic_update_slice x8, local copies, waits for them, and re-layouts, local(): query_grad, key_terms = lax.scan(back_step, zero_query, back_inputs)  17.6 us
  transfers between devices with their start and end apart: 7, of which 6 were waited for; matrix products, arithmetic and copies ran while one was open for 5% of the time, Pallas kernels for 0%

commit v1 on v0

v1 whole, which is shorter than its diff:
```python
import jax
import jax.numpy as jnp
from jax import lax
from jax.experimental import pallas as pl
from jax.experimental.pallas import tpu as pltpu
from jax.sharding import PartitionSpec as P

D = 768
HD = 64
ROT = 16


norm_eps = 1e-05


def layer_norm(values, scale, shift):
    mean_value = jnp.mean(values, axis=-1, keepdims=True)
    centred = values - mean_value
    variance = jnp.mean(centred * centred, axis=-1, keepdims=True)
    inv_std = lax.rsqrt(variance + norm_eps)
    normal_part = centred * inv_std
    return (normal_part * scale + shift, normal_part, inv_std)


def norm_backward(grad_normed, normal_part, inv_std, scale):
    grad_hat = grad_normed * scale
    mean_grad = jnp.mean(grad_hat, axis=-1, keepdims=True)
    mean_mixed = jnp.mean(grad_hat * normal_part, axis=-1, keepdims=True)
    return inv_std * (grad_hat - mean_grad - normal_part * mean_mixed)


def rotary_tables(positions):
    freqs = 10000.0 ** (-jnp.arange(0, ROT, 2).astype(jnp.float32) / ROT)
    angles = positions.astype(jnp.float32)[:, None] * freqs[None, :]
    angles = jnp.concatenate([angles, angles], axis=1)
    return (jnp.cos(angles), jnp.sin(angles))


def rotate(tensor, cosines, sines):
    part = tensor[..., :ROT]
    half = ROT // 2
    turned = jnp.concatenate([-part[..., half:], part[..., :half]], axis=-1)
    spun = part * cosines + turned * sines
    return jnp.concatenate([spun, tensor[..., ROT:]], axis=-1)


def gelu_grad(pre_act):
    cumulative = 0.5 * (1.0 + jax.scipy.special.erf(pre_act * 0.7071067811865476))
    density = jnp.exp(-0.5 * pre_act * pre_act) * 0.3989422804014327
    return cumulative + pre_act * density


NEG = -1e30
CONTRACT_LAST = (((1,), (1,)), ((), ()))
CONTRACT_FIRST = (((0,), (0,)), ((), ()))


def attention_kernel(bounds, first_ref, q_ref, g_ref, kv_ref, att_ref, dq_ref, dkv_ref):
    low, own = bounds[0], bounds[1]
    rows = q_ref.shape[1]
    queries = q_ref[0]
    grads = g_ref[0]
    first_key = first_ref[...]
    query_pos = own * rows + lax.broadcasted_iota(jnp.int32, (rows, 1), 0)

    def masked_scores(j, block):
        scores = lax.dot_general(queries, block, CONTRACT_LAST, preferred_element_type=jnp.float32)
        key_pos = j * rows + lax.broadcasted_iota(jnp.int32, (1, rows), 1)
        visible = (key_pos <= query_pos) & (key_pos >= first_key)
        return jnp.where(visible, scores, NEG), visible

    def forward(j, state):
        row_max, row_sum, total = state
        block = kv_ref[j, 0]
        scores, visible = masked_scores(j, block)
        new_max = jnp.maximum(row_max, jnp.max(scores, axis=1, keepdims=True))
        weights = jnp.where(visible, jnp.exp(scores - new_max), 0.0)
        factor = jnp.exp(row_max - new_max)
        row_sum = row_sum * factor + jnp.sum(weights, axis=1, keepdims=True)
        total = total * factor + jnp.dot(
            weights.astype(jnp.bfloat16), block, preferred_element_type=jnp.float32
        )
        return new_max, row_sum, total

    row_max, row_sum, total = lax.fori_loop(
        low,
        own + 1,
        forward,
        (
            jnp.full((rows, 1), NEG, jnp.float32),
            jnp.zeros((rows, 1), jnp.float32),
            jnp.zeros((rows, 2 * HD), jnp.float32),
        ),
    )
    attended = (total / row_sum).astype(jnp.bfloat16)
    att_ref[0] = attended
    log_total = row_max + jnp.log(row_sum)
    delta = jnp.sum(
        grads.astype(jnp.float32) * attended.astype(jnp.float32), axis=1, keepdims=True
    )
    dkv_ref[...] = jnp.zeros_like(dkv_ref)

    def backward(j, query_grad):
        block = kv_ref[j, 0]
        scores, visible = masked_scores(j, block)
        weights = jnp.where(visible, jnp.exp(scores - log_total), 0.0)
        grad_weights = lax.dot_general(
            grads, block, CONTRACT_LAST, preferred_element_type=jnp.float32
        )
        grad_scores = (weights * (grad_weights - delta)).astype(jnp.bfloat16)
        dkv = lax.dot_general(
            grad_scores, queries, CONTRACT_FIRST, preferred_element_type=jnp.float32
        ) + lax.dot_general(
            weights.astype(jnp.bfloat16), grads, CONTRACT_FIRST, preferred_element_type=jnp.float32
        )
        dkv_ref[j, 0] = dkv.astype(jnp.bfloat16)
        return query_grad + jnp.dot(grad_scores, block, preferred_element_type=jnp.float32)

    dq_ref[0] = lax.fori_loop(low, own + 1, backward, jnp.zeros((rows, 2 * HD), jnp.float32))


def attention(bounds, first_key, queries, grads, key_values):
    heads, rows, lanes = queries.shape
    blocks = key_values.shape[0]
    per_head = pl.BlockSpec((1, rows, lanes), lambda h, b: (h, 0, 0))
    all_blocks = pl.BlockSpec((blocks, 1, rows, lanes), lambda h, b: (0, h, 0, 0))
    return pl.pallas_call(
        attention_kernel,
        grid_spec=pltpu.PrefetchScalarGridSpec(
            num_scalar_prefetch=1,
            grid=(heads,),
            in_specs=[
                pl.BlockSpec((rows, 1), lambda h, b: (0, 0)),
                per_head,
                per_head,
                all_blocks,
            ],
            out_specs=[per_head, per_head, all_blocks],
        ),
        out_shape=[
            jax.ShapeDtypeStruct(queries.shape, jnp.bfloat16),
            jax.ShapeDtypeStruct(queries.shape, jnp.float32),
            jax.ShapeDtypeStruct(key_values.shape, jnp.bfloat16),
        ],
        cost_estimate=pl.CostEstimate(
            flops=14 * heads * rows * rows * blocks * lanes,
            bytes_accessed=4 * heads * rows * blocks * lanes,
            transcendentals=2 * heads * rows * rows * blocks,
        ),
    )(bounds, first_key, queries, grads, key_values)


def local(
    inputs,
    positions,
    attn_scale,
    attn_shift,
    mlp_scale,
    mlp_shift,
    qkv_weight,
    qv_bias,
    dense_weight,
    dense_bias,
    up_weight,
    up_bias,
    down_weight,
    down_bias,
    cotangent,
):
    f32, bf16 = jnp.float32, jnp.bfloat16
    local_width = qkv_weight.shape[2]
    hidden = up_weight.shape[1]
    heads = local_width // HD
    score_scale = HD ** (-0.5)
    own_rows = inputs.shape[0]
    tp_index = lax.axis_index("tp")
    ctx_index = lax.axis_index("ctx")
    both = lax.all_gather(
        jnp.concatenate([inputs, cotangent], axis=1), "tp", axis=0, tiled=True
    )
    rows = both.shape[0]
    grad_full = both[:, D:]
    normed_one, hat_one, std_one = layer_norm(both[:, :D].astype(f32), attn_scale, attn_shift)
    normed_two = hat_one * mlp_scale + mlp_shift
    attn_in = normed_one.astype(bf16)
    mlp_in = normed_two.astype(bf16)
    proj = jnp.dot(
        attn_in, qkv_weight.reshape(D, 3 * local_width), preferred_element_type=f32
    )
    proj = jnp.transpose(proj.reshape(rows, 3, heads, HD), (1, 2, 0, 3))
    cosines, sines = rotary_tables(positions)
    biases = qv_bias.reshape(2, heads, 1, HD)
    queries = rotate(proj[0] + biases[0], cosines, sines).astype(bf16) * bf16(score_scale)
    keys_rot = rotate(proj[1], cosines, sines).astype(bf16)
    values = (proj[2] + biases[1]).astype(bf16)
    own_kv = jnp.concatenate([keys_rot, values], axis=2)
    key_values = lax.all_gather(own_kv, "ctx", axis=0, tiled=False)

    grad_attended = jnp.dot(grad_full, dense_weight.T, preferred_element_type=f32).astype(bf16)
    grad_attended = jnp.transpose(grad_attended.reshape(rows, heads, HD), (1, 0, 2))
    blank = jnp.zeros((heads, rows, HD), bf16)
    padded_queries = jnp.concatenate([queries, blank], axis=2)
    padded_grads = jnp.concatenate([blank, grad_attended], axis=2)
    first_key = ctx_index * rows + jnp.arange(rows, dtype=jnp.int32) - positions
    bounds = jnp.stack([jnp.min(first_key) // rows, ctx_index]).astype(jnp.int32)

    pre_act = jnp.dot(mlp_in, up_weight, preferred_element_type=f32) + up_bias
    activation = jax.nn.gelu(pre_act, approximate=False).astype(bf16)
    mlp_part = jnp.dot(activation, down_weight, preferred_element_type=f32)
    grad_down = jnp.dot(activation.T, grad_full, preferred_element_type=f32)
    grad_act = jnp.dot(grad_full, down_weight.T, preferred_element_type=f32)
    grad_pre = grad_act * gelu_grad(pre_act)
    grad_up_bias = jnp.sum(grad_pre, axis=0)
    grad_pre_low = grad_pre.astype(bf16)
    grad_up = jnp.dot(mlp_in.T, grad_pre_low, preferred_element_type=f32)
    grad_mlp_in = jnp.dot(grad_pre_low, up_weight.T, preferred_element_type=f32)
    early = jnp.concatenate(
        [grad_up.astype(bf16).reshape(-1, D), grad_down.astype(bf16)], axis=0
    )
    early_low = lax.psum(early, "ctx")

    attended, query_grad, key_terms = attention(
        bounds, first_key[:, None], padded_queries, padded_grads, key_values
    )
    own_terms = lax.psum_scatter(key_terms, "ctx", scatter_dimension=0, tiled=True)[0]
    own_terms = own_terms.astype(f32)
    attended_flat = jnp.transpose(attended[:, :, HD:], (1, 0, 2)).reshape(rows, local_width)
    attn_part = jnp.dot(attended_flat, dense_weight, preferred_element_type=f32)
    grad_dense = jnp.dot(attended_flat.T, grad_full, preferred_element_type=f32)
    own_sums = lax.psum_scatter(
        jnp.concatenate([(attn_part + mlp_part).astype(bf16), grad_mlp_in.astype(bf16)], axis=1),
        "tp",
        scatter_dimension=0,
        tiled=True,
    ).astype(f32)
    branch_sum, own_mlp = own_sums[:, :D], own_sums[:, D:]
    resid = inputs.astype(f32)
    output = (resid + branch_sum + dense_bias + down_bias).astype(bf16)

    grad_query_pre = rotate(query_grad[:, :, :HD] * score_scale, cosines, -sines)
    grad_key_pre = rotate(own_terms[:, :, :HD], cosines, -sines)
    value_grad = own_terms[:, :, HD:]
    grad_proj = jnp.stack([grad_query_pre, grad_key_pre, value_grad]).astype(bf16)
    grad_proj = jnp.transpose(grad_proj, (2, 0, 1, 3)).reshape(rows, 3 * local_width)
    grad_attn_in = jnp.dot(
        grad_proj, qkv_weight.reshape(D, 3 * local_width).T, preferred_element_type=f32
    )
    own_attn = lax.psum_scatter(
        grad_attn_in.astype(bf16), "tp", scatter_dimension=0, tiled=True
    ).astype(f32)
    grad_qkv = jnp.dot(attn_in.T, grad_proj, preferred_element_type=f32)
    late = jnp.concatenate(
        [grad_qkv.astype(bf16).reshape(-1, D), grad_dense.astype(bf16)], axis=0
    )
    late, early_low = lax.optimization_barrier((late, early_low))
    early_sum = early_low.astype(f32)
    late_sum = lax.psum(late, "ctx").astype(f32)

    grad_out = cotangent.astype(f32)
    small = jnp.concatenate(
        [
            jnp.sum(grad_attn_in * hat_one, axis=0),
            jnp.sum(grad_attn_in, axis=0),
            jnp.sum(grad_mlp_in * hat_one, axis=0),
            jnp.sum(grad_mlp_in, axis=0),
            jnp.sum(grad_out, axis=0),
            jnp.sum(grad_query_pre, axis=1).reshape(-1),
            jnp.sum(value_grad, axis=1).reshape(-1),
            grad_up_bias,
        ]
    )
    gathered = lax.all_gather(small[None], ("ctx", "tp"), axis=0, tiled=True)
    shared = jnp.sum(gathered[:, : 5 * D], axis=0).reshape(5, D)
    per_tp = jnp.sum(gathered[:, 5 * D :].reshape(-1, lax.axis_size("tp"), 2 * local_width + hidden), axis=0)
    mine = lax.dynamic_index_in_dim(per_tp, tp_index, 0, keepdims=False)

    hat = lax.dynamic_slice_in_dim(hat_one, tp_index * own_rows, own_rows, 0)
    std = lax.dynamic_slice_in_dim(std_one, tp_index * own_rows, own_rows, 0)
    grad_input = grad_out + norm_backward(own_attn, hat, std, attn_scale)
    grad_input = grad_input + norm_backward(own_mlp, hat, std, mlp_scale)
    qkv_rows = late_sum.shape[0] - local_width
    up_rows = early_sum.shape[0] - hidden
    return (
        output,
        grad_input,
        shared[0],
        shared[1],
        shared[2],
        shared[3],
        late_sum[:qkv_rows].reshape(D, 3, local_width),
        mine[: 2 * local_width].reshape(2, local_width),
        late_sum[qkv_rows:],
        shared[4],
        early_sum[:up_rows].reshape(D, hidden),
        mine[2 * local_width :],
        early_sum[up_rows:],
        shared[4],
    )


def solution(mesh):
    in_specs = (
        P(("ctx", "tp"), None),
        P("ctx"),
        P(),
        P(),
        P(),
        P(),
        P(None, None, "tp"),
        P(None, "tp"),
        P("tp", None),
        P(),
        P(None, "tp"),
        P("tp"),
        P("tp", None),
        P(),
        P(("ctx", "tp"), None),
    )
    out_specs = (
        P(("ctx", "tp"), None),
        P(("ctx", "tp"), None),
        P(),
        P(),
        P(),
        P(),
        P(None, None, "tp"),
        P(None, "tp"),
        P("tp", None),
        P(),
        P(None, "tp"),
        P("tp"),
        P("tp", None),
        P(),
    )
    return jax.shard_map(local, mesh=mesh, in_specs=in_specs, out_specs=out_specs, check_vma=False)
```

time: 692 us -> 545 us (0.79)
  waiting for transfers between devices: 460 us -> 352 us
  blocking collectives: 91.2 us -> 42.2 us
  loops' own time: 16 us -> 0 us
  other arithmetic: 20.3 us -> 33.6 us
  Pallas kernels: 0 us -> 10.9 us
  matrix products: 33.3 us -> 24.3 us
  local copies, waits for them, and re-layouts: 54.8 us -> 61.8 us
    psum x2 -> x0, blocking collectives: 63.6 us -> none  [the longest x1 43 us: local(): lax.psum((jnp.sum(own_attn * hat_one, axis=0), jnp.sum(own_attn, axis=0),...]
    reduce_scatter x4 -> x3, waiting for transfers between devices: 189 us -> 133 us  [the longest x1 88.5 us: local(): lax.psum_scatter(key_terms, 'ctx', scatter_dimension=0, tiled=True)[0]]
    psum x1 -> x2, waiting for transfers between devices: 193 us -> 152 us  [the longest x1 85.5 us: local(): early_low = lax.psum(early, 'ctx')]
    dynamic_update_slice x8 -> x0, local copies, waits for them, and re-layouts: 17.6 us -> none  [local(): query_grad, key_terms = lax.scan(back_step, zero_query, back_inputs)]
    another operation x10 -> x0, loops' own time: 16 us -> none  [the longest x1 7.94 us: local(): query_grad, key_terms = lax.scan(back_step, zero_query, back_inputs)]
    all_gather x3 -> x1, blocking collectives: 27.5 us -> 42.2 us  [local(): gathered = lax.all_gather(small[None], ('ctx', 'tp'), axis=0, tiled=True)]
    all_gather x2, waiting for transfers between devices: 77.6 us -> 66.4 us  [the longest x1 48.2 us: local(): key_values = lax.all_gather(own_kv, 'ctx', axis=0, tiled=False)]
    pallas_call x0 -> x1, Pallas kernels: none -> 10.9 us  [attention(): pl.pallas_call(attention_kernel, grid_spec=pltpu.PrefetchScalarGridSpec(n...]
  transfers between devices with their start and end apart: 7 -> 7, of which waited for: 6 -> 7; matrix products, arithmetic and copies ran while one was open for 5% -> 15% of each run, Pallas kernels for 0% -> 0%
where the time goes in v1:
time: 545 us; the launch traced here: 543 us
  waiting for transfers between devices  352 us (65%)
  local copies, waits for them, and re-layouts  61.8 us (11%)
  blocking collectives  42.2 us (8%)
  other arithmetic  33.6 us (6%)
  matrix products  24.3 us (4%)
  between operations  17.3 us (3%)
  Pallas kernels  10.9 us (2%)
    reduce_scatter x1, waiting for transfers between devices, local(): lax.psum_scatter(key_terms, 'ctx', scatter_dimension=0, tiled=True)[0]  88.5 us
    psum x1, waiting for transfers between devices, local(): early_low = lax.psum(early, 'ctx')  85.5 us
    psum x1, waiting for transfers between devices, local(): late_sum = lax.psum(late, 'ctx').astype(f32)  66.3 us
    all_gather x1, waiting for transfers between devices, local(): key_values = lax.all_gather(own_kv, 'ctx', axis=0, tiled=False)  48.2 us
    all_gather x1, blocking collectives, local(): gathered = lax.all_gather(small[None], ('ctx', 'tp'), axis=0, tiled=True)  42.2 us
    reduce_scatter x1, waiting for transfers between devices, local(): lax.psum_scatter(grad_attn_in.astype(bf16), 'tp', scatter_dimension=0, ti...  24.7 us
    reduce_scatter x1, waiting for transfers between devices, local(): lax.psum_scatter(jnp.concatenate([(attn_part + mlp_part).astype(bf16), gr...  20 us
    all_gather x1, waiting for transfers between devices, local(): lax.all_gather(jnp.concatenate([inputs, cotangent], axis=1), 'tp', axis=0...  18.2 us
  transfers between devices with their start and end apart: 7, of which 7 were waited for; matrix products, arithmetic and copies ran while one was open for 15% of the time, Pallas kernels for 0%

profile of v1, /device:TPU:0, one launch (start us, length us, event | category | flops | bytes accessed | tf_op | source)
XLA Modules:
  0.0 543.1 jit_solution(7888175637497601443)
XLA Ops:
  7.3 1.9 pad_maximum_fusion.4
  11.4 1.4 fusion.47
  14.4 18.2 %all-gather.6.cloned.1.call-done = bf16[512,1536]{1,0:T(8,128)(2,1)} async-done(((bf16[128,1536]{1,0:T(8,128)(2,1)}), bf16[512,1536]{1,0:T(8,128)(2,1)}) %all-gather.6.cloned.1.call-update) | async-done | bytes 1572880 | tf_op jit(solution)/shard_map/all_gather | solution.py:178
  32.6 1.4 convert_reduce_fusion
  34.0 1.5 fusion.2
  35.6 1.3 convolution_bitcast_fusion
  39.9 1.4 slice_negate_fusion.3
  41.3 2.0 copy.65
  43.3 2.0 copy.66
  45.3 2.0 copy.71
  48.1 1.6 maximum_multiply_fusion.2
  50.8 2.0 copy.69
  52.9 2.2 fusion.24
  61.3 2.1 convolution_convert_fusion.4
  63.4 1.9 copy.70
  65.3 1.9 concatenate.69.g_ref
  68.3 48.2 %all-gather.8.cloned.1.call-done = bf16[24,512,128]{2,1,0:T(8,128)(2,1)} async-done(((bf16[3,512,128]{2,1,0:T(8,128)(2,1)}), bf16[24,512,128]{2,1,0:T(8,128)(2,1)}) %all-gather.8.cloned.1.call-update) | async-done | bytes 3145744 | tf_op jit(solution)/shard_map/all_gather | solution.py:197
  116.4 10.9 %shard_map.254 = (bf16[3,512,128]{2,1,0:T(8,128)(2,1)}, f32[3,512,128]{2,1,0:T(8,128)}, bf16[8,3,512,128]{3,2,1,0:T(8,128)(2,1)}) custom-call(s32[2]{0:T(128)} %pad_add_fusion.bounds, s32[512,1]{1,0:T(8,128)} %copy.75.first_ref, bf16[3,512,128]{2,1,0:T(8,128)(2,1)} %concatenate.68.q_ref, bf16[3,512,128]{2,1,0:T(8,128)(2,1)} %concatenate.69.g_ref, ...), custom_call_target="tpu_custom_call" | custom-call | flops 11274289152 | bytes 6291456 | tf_op jit(solution)/shard_map/pallas_call | solution.py:127
  128.1 4.0 fusion.5
  133.7 1.7 fusion.50
  137.3 1.6 pad_maximum_fusion
  146.2 2.6 fusion.51
  148.9 88.5 %reduce-scatter.6.cloned.1.call-done = bf16[1,3,512,128]{3,2,1,0:T(8,128)(2,1)} async-done(((bf16[8,3,512,128]{3,2,1,0:T(8,128)(2,1)}), bf16[1,3,512,128]{3,2,1,0:T(8,128)(2,1)}) %reduce-scatter.6.cloned.1.call-update) | async-done | bytes 393232 | tf_op jit(solution)/shard_map/reduce_scatter | solution.py:225
  237.3 1.9 slice.212
  241.4 2.0 copy.82
  246.3 1.2 copy.85
  247.6 1.7 fusion.20
  250.0 1.3 maximum_bitcast_fusion
  251.3 1.5 copy.86
  252.8 2.9 convolution_convert_fusion.2
  255.7 2.2 copy.87
  257.9 3.2 reshape.211
  261.2 2.4 pad_maximum_fusion.2
  263.5 85.5 %all-reduce.5.cloned.1.call-done = bf16[1536,768]{1,0:T(8,128)(2,1)} async-done(((bf16[1536,768]{1,0:T(8,128)(2,1)}), bf16[1536,768]{1,0:T(8,128)(2,1)}) %all-reduce.5.cloned.1.call-update) | async-done | bytes 2359312 | tf_op jit(solution)/shard_map/psum | solution.py:220
  349.2 2.9 add_convert_fusion
  353.6 3.0 multiply_reduce_fusion
  356.7 1.3 pad_maximum_fusion.1
  358.8 1.3 dynamic-slice.3
  361.4 4.2 fusion.48
  365.6 66.3 %all-reduce.7.cloned.1.call-done = bf16[768,768]{1,0:T(8,128)(2,1)} async-done(((bf16[768,768]{1,0:T(8,128)(2,1)}), bf16[768,768]{1,0:T(8,128)(2,1)}) %all-reduce.7.cloned.1.call-update) | async-done | bytes 1179664 | tf_op jit(solution)/shard_map/psum | solution.py:257
  431.9 1.3 slice.220
  433.2 3.1 reshape.212
  436.3 4.4 copy.88
  441.6 20.0 %reduce-scatter.4.cloned.1.call-done = bf16[128,1536]{1,0:T(8,128)(2,1)} async-done(((bf16[512,1536]{1,0:T(8,128)(2,1)}), bf16[128,1536]{1,0:T(8,128)(2,1)}) %reduce-scatter.4.cloned.1.call-update) | async-done | bytes 393232 | tf_op jit(solution)/shard_map/reduce_scatter | solution.py:230
  462.6 24.7 %reduce-scatter.8.cloned.1.call-done = bf16[128,768]{1,0:T(8,128)(2,1)} async-done(((bf16[512,768]{1,0:T(8,128)(2,1)}), bf16[128,768]{1,0:T(8,128)(2,1)}) %reduce-scatter.8.cloned.1.call-update) | async-done | bytes 196624 | tf_op jit(solution)/shard_map/reduce_scatter | solution.py:248
  487.4 1.4 multiply_reduce_fusion.3
  488.8 2.2 fusion.33
  491.2 42.2 %all-gather.2 = f32[32,1,4992]{2,1,0:T(1,128)S(1)} all-gather(f32[1,1,4992]{2,1,0:T(1,128)S(1)} %reshape.217), channel_id=3, replica_groups=mesh['ctx'=8,'tp'=4] {'ctx','tp'}, dimensions={0}, use_global_device_ids=true | all-gather | bytes 658944 | tf_op jit(solution)/shard_map/all_gather | solution.py:272
  (161 shorter events, 39.2 us)
Async XLA Ops:
  7.2 120.4 %copy-start = (bf16[768,768]{1,0:T(8,128)(2,1)S(1)}, bf16[768,768]{1,0:T(8,128)(2,1)}, u32[]{:S(2)}) copy-start(bf16[768,768]{1,0:T(8,128)(2,1)} %param.25) | copy-start | bytes 3538948
  7.2 28.3 %copy-start.22 = (f32[768]{0:T(1024)S(1)}, f32[768]{0:T(1024)}, u32[]{:S(2)}) copy-start(f32[768]{0:T(1024)} %param.17) | copy-start | bytes 9220
  7.2 28.3 %copy-start.40 = (f32[768]{0:T(1024)S(1)}, f32[768]{0:T(1024)}, u32[]{:S(2)}) copy-start(f32[768]{0:T(1024)} %param.18) | copy-start | bytes 9220
  7.2 28.3 %copy-start.13 = (bf16[768,3,192]{0,2,1:T(8,128)(2,1)S(1)}, bf16[768,3,192]{0,2,1:T(8,128)(2,1)}, u32[]{:S(2)}) copy-start(bf16[768,3,192]{0,2,1:T(8,128)(2,1)} %param.21) | copy-start | bytes 2654212
  7.2 25.3 %all-gather.6.cloned.1.call-start = ((), (), s32[]{:S(2)}) async-start(), calls=%async_computation.3 | async-start | bytes 1966080 | tf_op jit(solution)/shard_map/all_gather | solution.py:178
  9.2 107.2 %all-gather.8.cloned.1.call-start = ((), (), s32[]{:S(2)}) async-start(), calls=%async_computation.9 | async-start | bytes 3538944 | tf_op jit(solution)/shard_map/all_gather | solution.py:197
  32.6 3.0 copy-start.4
  35.5 217.3 %copy-start.28 = (f32[512]{0:T(512)}, f32[512]{0:T(512)S(1)}, u32[]{:S(2)}) copy-start(f32[512]{0:T(512)S(1)} %add_rsqrt_fusion) | copy-start | bytes 6148
  37.9 1.2 copy-start.30
  37.9 1.2 copy-start.31
  52.9 2.2 copy-start.10
  52.9 2.2 copy-start.12
  55.1 6.2 %copy-start.5 = (bf16[512,1536]{1,0:T(8,128)(2,1)S(1)}, bf16[512,1536]{1,0:T(8,128)(2,1)}, u32[]{:S(2)}) copy-start(bf16[512,1536]{1,0:T(8,128)(2,1)} %all-gather.6.cloned.1.call-done) | copy-start | bytes 4718596
  56.3 181.1 %reduce-scatter.6.cloned.1.call-start = ((), (), s32[]{:S(2)}) async-start(), calls=%async_computation.5 | async-start | bytes 3538944 | tf_op jit(solution)/shard_map/reduce_scatter | solution.py:225
  61.3 5.9 %copy-start.8 = (bf16[3,512,16]{2,1,0:T(8,128)(2,1)S(1)}, bf16[3,512,16]{2,1,0:T(8,128)(2,1)}, u32[]{:S(2)}) copy-start(bf16[3,512,16]{2,1,0:T(8,128)(2,1)} %get-tuple-element.98) | copy-start | bytes 147460
  61.3 5.9 %copy-start.11 = (bf16[3,512,48]{2,1,0:T(8,128)(2,1)S(1)}, bf16[3,512,48]{2,1,0:T(8,128)(2,1)}, u32[]{:S(2)}) copy-start(bf16[3,512,48]{2,1,0:T(8,128)(2,1)} %slice.304) | copy-start | bytes 442372
  127.3 0.7 copy-start.38
  127.3 0.7 copy-start.39
  127.4 221.7 %all-reduce.5.cloned.1.call-start = ((), (), s32[]{:S(2)}) async-start(), calls=%async_computation.7 | async-start | bytes 4718592 | tf_op jit(solution)/shard_map/psum | solution.py:220
  132.1 1.0 copy-start.42
  132.1 1.6 copy-start.37
  135.4 0.9 copy-start.15
  138.8 1.0 copy-start.21
  138.8 2.0 copy-start.17
  138.9 293.0 %all-reduce.7.cloned.1.call-start = ((), (), s32[]{:S(2)}) async-start(), calls=%async_computation.8 | async-start | bytes 2359296 | tf_op jit(solution)/shard_map/psum | solution.py:257
  140.9 1.4 copy-start.6
  140.9 1.4 copy-start.20
  247.6 1.7 copy-start.1
  247.6 1.8 copy-start.9
  249.9 2.9 copy-start.41
  349.1 112.5 %reduce-scatter.4.cloned.1.call-start = ((), (), s32[]{:S(2)}) async-start(), calls=%async_computation.4 | async-start | bytes 1966080 | tf_op jit(solution)/shard_map/reduce_scatter | solution.py:230
  349.1 2.9 copy-start.14
  352.0 1.4 copy-start.7
  352.0 1.6 copy-start.16
  352.0 1.6 copy-start.29
  358.0 3.0 copy-start.2
  358.0 129.3 %reduce-scatter.8.cloned.1.call-start = ((), (), s32[]{:S(2)}) async-start(), calls=%async_computation.6 | async-start | bytes 983040 | tf_op jit(solution)/shard_map/reduce_scatter | solution.py:248
  436.3 4.4 copy-start.3
  440.7 48.1 %copy-start.18 = (bf16[128,768]{1,0:T(8,128)(2,1)S(1)}, bf16[128,768]{1,0:T(8,128)(2,1)}, u32[]{:S(2)}) copy-start(bf16[128,768]{1,0:T(8,128)(2,1)} %param.29) | copy-start | bytes 589828
  440.7 48.1 %copy-start.19 = (bf16[128,768]{1,0:T(8,128)(2,1)S(1)}, bf16[128,768]{1,0:T(8,128)(2,1)}, u32[]{:S(2)}) copy-start(bf16[128,768]{1,0:T(8,128)(2,1)} %param.15) | copy-start | bytes 589828
  440.7 48.1 %copy-start.32 = (f32[768]{0:T(1024)S(1)}, f32[768]{0:T(1024)}, u32[]{:S(2)}) copy-start(f32[768]{0:T(1024)} %param.28) | copy-start | bytes 9220
  440.7 48.1 %copy-start.33 = (f32[768]{0:T(1024)S(1)}, f32[768]{0:T(1024)}, u32[]{:S(2)}) copy-start(f32[768]{0:T(1024)} %param.24) | copy-start | bytes 9220
  440.7 48.1 %copy-start.36 = (f32[128]{0:T(128)S(1)}, f32[128]{0:T(128)}, u32[]{:S(2)}) copy-start(f32[128]{0:T(128)} %dynamic-slice.3) | copy-start | bytes 1540
  487.3 3.7 copy-start.24
  487.3 3.7 copy-start.25
  487.4 3.7 copy-start.26
  487.4 3.7 copy-start.34
  487.4 3.7 copy-start.35
  (2 other events, 1.3 us)
Sparse Core Ops, SparseCore 0:
  10.2 22.3 all-gather.5
  56.4 60.0 all-gather.7
  127.5 109.7 reduce-scatter.5
  241.3 107.7 all-reduce.4
  352.4 79.4 all-reduce.6
  434.3 27.2 reduce-scatter.3
  464.1 23.1 reduce-scatter.7

commit v2 on v1

--- a/solution.py
+++ b/solution.py
@@ -31,17 +31,18 @@
 
 def rotary_tables(positions):
     freqs = 10000.0 ** (-jnp.arange(0, ROT, 2).astype(jnp.float32) / ROT)
-    angles = positions.astype(jnp.float32)[:, None] * freqs[None, :]
-    angles = jnp.concatenate([angles, angles], axis=1)
-    return (jnp.cos(angles), jnp.sin(angles))
+    angles = positions.astype(jnp.float32)[:, None] * jnp.tile(freqs, HD // (ROT // 2))[None, :]
+    spun = (jnp.arange(HD) < ROT)[None, :]
+    return (jnp.where(spun, jnp.cos(angles), 1.0), jnp.where(spun, jnp.sin(angles), 0.0))
 
 
 def rotate(tensor, cosines, sines):
-    part = tensor[..., :ROT]
     half = ROT // 2
-    turned = jnp.concatenate([-part[..., half:], part[..., :half]], axis=-1)
-    spun = part * cosines + turned * sines
-    return jnp.concatenate([spun, tensor[..., ROT:]], axis=-1)
+    source, target = jnp.arange(HD)[:, None], jnp.arange(HD)[None, :]
+    swap = jnp.where((target < half) & (source == target + half), -1.0, 0.0)
+    swap += jnp.where((target >= half) & (target < ROT) & (source == target - half), 1.0, 0.0)
+    turned = jnp.dot(tensor, swap, precision=lax.Precision.HIGHEST)
+    return tensor * cosines + turned * sines
 
 
 def gelu_grad(pre_act):
@@ -217,26 +218,18 @@
     early = jnp.concatenate(
         [grad_up.astype(bf16).reshape(-1, D), grad_down.astype(bf16)], axis=0
     )
+    key_values, early = lax.optimization_barrier((key_values, early))
     early_low = lax.psum(early, "ctx")
 
     attended, query_grad, key_terms = attention(
         bounds, first_key[:, None], padded_queries, padded_grads, key_values
     )
+    key_terms, early_low = lax.optimization_barrier((key_terms, early_low))
     own_terms = lax.psum_scatter(key_terms, "ctx", scatter_dimension=0, tiled=True)[0]
     own_terms = own_terms.astype(f32)
     attended_flat = jnp.transpose(attended[:, :, HD:], (1, 0, 2)).reshape(rows, local_width)
     attn_part = jnp.dot(attended_flat, dense_weight, preferred_element_type=f32)
     grad_dense = jnp.dot(attended_flat.T, grad_full, preferred_element_type=f32)
-    own_sums = lax.psum_scatter(
-        jnp.concatenate([(attn_part + mlp_part).astype(bf16), grad_mlp_in.astype(bf16)], axis=1),
-        "tp",
-        scatter_dimension=0,
-        tiled=True,
-    ).astype(f32)
-    branch_sum, own_mlp = own_sums[:, :D], own_sums[:, D:]
-    resid = inputs.astype(f32)
-    output = (resid + branch_sum + dense_bias + down_bias).astype(bf16)
-
     grad_query_pre = rotate(query_grad[:, :, :HD] * score_scale, cosines, -sines)
     grad_key_pre = rotate(own_terms[:, :, :HD], cosines, -sines)
     value_grad = own_terms[:, :, HD:]
@@ -245,17 +238,10 @@
     grad_attn_in = jnp.dot(
         grad_proj, qkv_weight.reshape(D, 3 * local_width).T, preferred_element_type=f32
     )
-    own_attn = lax.psum_scatter(
-        grad_attn_in.astype(bf16), "tp", scatter_dimension=0, tiled=True
-    ).astype(f32)
     grad_qkv = jnp.dot(attn_in.T, grad_proj, preferred_element_type=f32)
     late = jnp.concatenate(
         [grad_qkv.astype(bf16).reshape(-1, D), grad_dense.astype(bf16)], axis=0
     )
-    late, early_low = lax.optimization_barrier((late, early_low))
-    early_sum = early_low.astype(f32)
-    late_sum = lax.psum(late, "ctx").astype(f32)
-
     grad_out = cotangent.astype(f32)
     small = jnp.concatenate(
         [
@@ -269,7 +255,18 @@
             grad_up_bias,
         ]
     )
+    late, small = lax.optimization_barrier((late, small))
     gathered = lax.all_gather(small[None], ("ctx", "tp"), axis=0, tiled=True)
+    branches = jnp.concatenate(
+        [part.astype(bf16) for part in (attn_part + mlp_part, grad_mlp_in, grad_attn_in)], axis=1
+    )
+    branches, gathered = lax.optimization_barrier((branches, gathered))
+    own_sums = lax.psum_scatter(branches, "tp", scatter_dimension=0, tiled=True).astype(f32)
+    branch_sum, own_mlp, own_attn = jnp.split(own_sums, 3, axis=1)
+    resid = inputs.astype(f32)
+    output = (resid + branch_sum + dense_bias + down_bias).astype(bf16)
+    early_sum = early_low.astype(f32)
+    late_sum = lax.psum(late, "ctx").astype(f32)
     shared = jnp.sum(gathered[:, : 5 * D], axis=0).reshape(5, D)
     per_tp = jnp.sum(gathered[:, 5 * D :].reshape(-1, lax.axis_size("tp"), 2 * local_width + hidden), axis=0)
     mine = lax.dynamic_index_in_dim(per_tp, tp_index, 0, keepdims=False)

time: 545 us -> 437 us (0.80)
  waiting for transfers between devices: 352 us -> 269 us
  local copies, waits for them, and re-layouts: 61.8 us -> 41.8 us
  other arithmetic: 33.6 us -> 22 us
  matrix products: 24.3 us -> 31.5 us
    psum x1, waiting for transfers between devices: 66.3 us -> 24.2 us  [local(): late_sum = lax.psum(late, 'ctx').astype(f32)]
    reduce_scatter x1, waiting for transfers between devices: 88.5 us -> 67.5 us  [local(): lax.psum_scatter(key_terms, 'ctx', scatter_dimension=0, tiled=True)[0]]
    reduce_scatter x2 -> x1, waiting for transfers between devices: 44.7 us -> 24.7 us  [local(): lax.psum_scatter(branches, 'tp', scatter_dimension=0, tiled=True)]
    slice x8 -> x0, local copies, waits for them, and re-layouts: 9.46 us -> none  [the longest x4 4.91 us: rotate(): return jnp.concatenate([spun, tensor[..., ROT:]], axis=-1)]
    dot_general x0 -> x4, matrix products: none -> 7.02 us  [rotate(): turned = jnp.dot(tensor, swap, precision=lax.Precision.HIGHEST)]
    neg x4 -> x0, local copies, waits for them, and re-layouts: 6.81 us -> none  [rotate(): turned = jnp.concatenate([-part[..., half:], part[..., :half]], axis=-1)]
    mul x4 -> x1, local copies, waits for them, and re-layouts: 5.59 us -> 0.08 us  [rotary_tables(): positions.astype(jnp.float32)[:, None]]
  transfers between devices with their start and end apart: 7 -> 6, of which waited for: 7 -> 6; matrix products, arithmetic and copies ran while one was open for 15% -> 13% of each run, Pallas kernels for 0% -> 3%
where the time goes in v2:
time: 437 us; the launch traced here: 436 us
  waiting for transfers between devices  269 us (62%)
  blocking collectives  43.3 us (10%)
  local copies, waits for them, and re-layouts  41.8 us (10%)
  matrix products  31.5 us (7%)
  other arithmetic  22 us (5%)
  between operations  17.2 us (4%)
  Pallas kernels  10.9 us (2%)
    psum x1, waiting for transfers between devices, local(): early_low = lax.psum(early, 'ctx')  86.7 us
    reduce_scatter x1, waiting for transfers between devices, local(): lax.psum_scatter(key_terms, 'ctx', scatter_dimension=0, tiled=True)[0]  67.5 us
    all_gather x1, waiting for transfers between devices, local(): key_values = lax.all_gather(own_kv, 'ctx', axis=0, tiled=False)  48.5 us
    all_gather x1, blocking collectives, local(): gathered = lax.all_gather(small[None], ('ctx', 'tp'), axis=0, tiled=True)  43.3 us
    reduce_scatter x1, waiting for transfers between devices, local(): lax.psum_scatter(branches, 'tp', scatter_dimension=0, tiled=True)  24.7 us
    psum x1, waiting for transfers between devices, local(): late_sum = lax.psum(late, 'ctx').astype(f32)  24.2 us
    all_gather x1, waiting for transfers between devices, local(): lax.all_gather(jnp.concatenate([inputs, cotangent], axis=1), 'tp', axis=0...  17 us
    pallas_call x1, Pallas kernels, attention(): pl.pallas_call(attention_kernel, grid_spec=pltpu.PrefetchScalarGridSpec(n...  10.9 us
  transfers between devices with their start and end apart: 6, of which 6 were waited for; matrix products, arithmetic and copies ran while one was open for 13% of the time, Pallas kernels for 3%

profile of v2, /device:TPU:0, one launch (start us, length us, event | category | flops | bytes accessed | tf_op | source)
XLA Modules:
  0.0 436.2 jit_solution(18020830448423003297)
XLA Ops:
  7.2 1.9 pad_maximum_fusion.3
  9.3 1.3 slice_reduce_fusion.2
  12.4 1.4 fusion.109
  13.8 1.8 broadcast_multiply_fusion
  15.5 17.0 %all-gather.6.cloned.1.call-done = bf16[512,1536]{1,0:T(8,128)(2,1)} async-done(((bf16[128,1536]{1,0:T(8,128)(2,1)}), bf16[512,1536]{1,0:T(8,128)(2,1)}) %all-gather.6.cloned.1.call-update) | async-done | bytes 1572880 | tf_op jit(solution)/shard_map/all_gather | solution.py:179
  32.5 1.4 convert_reduce_fusion
  34.0 1.5 fusion.2
  35.6 2.5 convolution_bitcast_fusion
  38.2 1.3 copy-done.12
  40.4 1.0 pad_maximum_fusion.4
  41.5 4.8 %fusion.10 = (bf16[512,768]{1,0:T(8,128)(2,1)S(1)}, f32[512,768]{1,0:T(8,128)S(1)}) fusion(f32[768]{0:T(1024)} %param.26, bf16[768,768]{1,0:T(8,128)(2,1)S(1)} %copy-done, f32[768]{0:T(1024)} %param.20, f32[768]{0:T(1024)S(1)} %copy-done.18, f32[512]{0:T(512)} %copy-done.20, f32[512]{0:T(512)S(1)} %broadcast_multiply_fusion.1, ...), kind=kOutput, calls=%fused_computation.17 | convolution fusion | flops 632291328 | bytes 4339712 | tf_op jit(solution)/shard_map/dot_general | solution.py:208
  47.8 1.7 fusion.113
  49.5 0.9 copy-done.13
  50.5 1.0 convolution_convert_fusion.1
  51.5 1.6 pad_maximum_fusion
  53.0 48.5 %all-gather.8.cloned.1.call-done = bf16[24,512,128]{2,1,0:T(8,128)(2,1)} async-done(((bf16[3,512,128]{2,1,0:T(8,128)(2,1)}), bf16[24,512,128]{2,1,0:T(8,128)(2,1)}) %all-gather.8.cloned.1.call-update) | async-done | bytes 3145744 | tf_op jit(solution)/shard_map/all_gather | solution.py:198
  104.4 1.3 add.174
  107.2 2.1 convolution_convert_fusion.4
  109.3 1.9 copy.71
  111.2 2.5 fusion.26
  114.5 0.9 concatenate.26.g_ref
  115.4 10.9 %shard_map.254 = (bf16[3,512,128]{2,1,0:T(8,128)(2,1)}, f32[3,512,128]{2,1,0:T(8,128)}, bf16[8,3,512,128]{3,2,1,0:T(8,128)(2,1)}) custom-call(s32[2]{0:T(128)} %pad_add_fusion.bounds, s32[512,1]{1,0:T(8,128)} %copy.74.first_ref, bf16[3,512,128]{2,1,0:T(8,128)(2,1)} %concatenate.25.q_ref, bf16[3,512,128]{2,1,0:T(8,128)(2,1)} %concatenate.26.g_ref, ...), custom_call_target="tpu_custom_call" | custom-call | flops 11274289152 | bytes 6291456 | tf_op jit(solution)/shard_map/pallas_call | solution.py:128
  126.4 86.7 %all-reduce.5.cloned.1.call-done = bf16[1536,768]{1,0:T(8,128)(2,1)} async-done(((bf16[1536,768]{1,0:T(8,128)(2,1)}), bf16[1536,768]{1,0:T(8,128)(2,1)}) %all-reduce.5.cloned.1.call-update) | async-done | bytes 2359312 | tf_op jit(solution)/shard_map/psum | solution.py:222
  214.6 3.1 fusion.111
  218.4 1.9 slice_bitcast_fusion.4
  220.3 1.1 copy.75
  221.5 1.0 convolution_convert_fusion.3
  222.5 67.5 %reduce-scatter.3.cloned.1.call-done = bf16[1,3,512,128]{3,2,1,0:T(8,128)(2,1)} async-done(((bf16[8,3,512,128]{3,2,1,0:T(8,128)(2,1)}), bf16[1,3,512,128]{3,2,1,0:T(8,128)(2,1)}) %reduce-scatter.3.cloned.1.call-update) | async-done | bytes 393232 | tf_op jit(solution)/shard_map/reduce_scatter | solution.py:228
  290.1 1.1 bitcast_convert_fusion
  293.9 2.1 fusion.119
  296.0 1.7 convolution_convert_fusion.2
  297.8 2.3 copy.82
  300.1 3.2 reshape.302
  303.3 2.3 pad_maximum_fusion.2
  305.5 4.4 %multiply_reduce_fusion = (f32[768]{0:T(1024)S(1)}, f32[768]{0:T(1024)}, f32[768]{0:T(1024)}, f32[768]{0:T(1024)}, f32[512,768]{1,0:T(8,128)}, /*index=5*/bf16[512,768]{1,0:T(8,128)(2,1)S(1)}, bf16[512,768]{1,0:T(8,128)(2,1)}) fusion(f32[512]{0:T(512)} %copy-done.20, f32[512]{0:T(512)S(1)} %broadcast_multiply_fusion.1, ...), kind=kOutput, calls=%fused_computation.18 | convolution fusion | flops 608302080 | bytes 7487488 | tf_op jit(solution)/shard_map/dot_general | solution.py:217
  311.1 1.5 fusion.118
  313.6 43.3 %all-gather.2 = f32[32,1,4992]{2,1,0:T(1,128)S(1)} all-gather(f32[1,1,4992]{2,1,0:T(1,128)S(1)} %reshape.310), channel_id=3, replica_groups=mesh['ctx'=8,'tp'=4] {'ctx','tp'}, dimensions={0}, use_global_device_ids=true | all-gather | bytes 658944 | tf_op jit(solution)/shard_map/all_gather | solution.py:259
  357.7 1.6 pad_maximum_fusion.1
  361.0 2.5 fusion.110
  363.6 0.9 slice.104
  365.3 1.1 slice_reduce_fusion.1
  367.6 24.2 %all-reduce.7.cloned.1.call-done = bf16[768,768]{1,0:T(8,128)(2,1)} async-done(((bf16[768,768]{1,0:T(8,128)(2,1)}), bf16[768,768]{1,0:T(8,128)(2,1)}) %all-reduce.7.cloned.1.call-update) | async-done | bytes 1179664 | tf_op jit(solution)/shard_map/psum | solution.py:269
  391.8 1.3 slice.124
  393.1 3.1 reshape.305
  396.2 4.4 %copy.83 = f32[768,3,192]{0,2,1:T(8,128)} copy(f32[768,3,192]{2,1,0:T(4,128)} %reshape.305) | data formatting | bytes 3538944
  401.5 24.7 %reduce-scatter.5.cloned.1.call-done = bf16[128,2304]{1,0:T(8,128)(2,1)} async-done(((bf16[512,2304]{1,0:T(8,128)(2,1)}), bf16[128,2304]{1,0:T(8,128)(2,1)}) %reduce-scatter.5.cloned.1.call-update) | async-done | bytes 589840 | tf_op jit(solution)/shard_map/reduce_scatter | solution.py:264
  426.2 1.1 convert_element_type.101
  427.7 1.1 fusion.38
  (133 shorter events, 20.2 us)
Async XLA Ops:
  7.2 34.3 %copy-start = (bf16[768,768]{1,0:T(8,128)(2,1)S(1)}, bf16[768,768]{1,0:T(8,128)(2,1)}, u32[]{:S(2)}) copy-start(bf16[768,768]{1,0:T(8,128)(2,1)} %param.25) | copy-start | bytes 3538948
  7.2 25.3 %all-gather.6.cloned.1.call-start = ((), (), s32[]{:S(2)}) async-start(), calls=%async_computation.2 | async-start | bytes 1966080 | tf_op jit(solution)/shard_map/all_gather | solution.py:179
  9.1 26.4 %copy-start.17 = (f32[768]{0:T(1024)S(1)}, f32[768]{0:T(1024)}, u32[]{:S(2)}) copy-start(f32[768]{0:T(1024)} %param.17) | copy-start | bytes 9220
  9.1 92.4 %all-gather.8.cloned.1.call-start = ((), (), s32[]{:S(2)}) async-start(), calls=%async_computation.7 | async-start | bytes 3538944 | tf_op jit(solution)/shard_map/all_gather | solution.py:198
  32.5 3.0 copy-start.3
  35.5 2.6 copy-start.20
  35.5 2.6 copy-start.23
  35.5 4.0 copy-start.24
  35.5 4.0 copy-start.26
  35.5 4.0 copy-start.28
  35.5 4.0 copy-start.30
  38.1 1.4 copy-start.12
  39.5 1.9 copy-start.18
  41.4 171.6 %all-reduce.5.cloned.1.call-start = ((), (), s32[]{:S(2)}) async-start(), calls=%async_computation.3 | async-start | bytes 4718592 | tf_op jit(solution)/shard_map/psum | solution.py:222
  46.3 0.9 copy-start.39
  46.3 1.6 copy-start.35
  47.8 2.6 copy-start.21
  47.8 2.6 copy-start.37
  49.5 0.9 copy-start.13
  101.6 188.5 %reduce-scatter.3.cloned.1.call-start = ((), (), s32[]{:S(2)}) async-start(), calls=%async_computation.4 | async-start | bytes 3538944 | tf_op jit(solution)/shard_map/reduce_scatter | solution.py:228
  106.6 4.6 %copy-start.34 = (f32[3,64]{1,0:T(4,128)S(1)}, f32[3,64]{1,0:T(4,128)}, u32[]{:S(2)}) copy-start(f32[3,64]{1,0:T(4,128)} %add.174) | copy-start | bytes 2308
  111.2 3.3 copy-start.10
  213.1 0.9 copy-start.7
  213.1 1.6 copy-start.25
  213.1 1.6 copy-start.27
  213.1 1.6 copy-start.29
  213.1 1.6 copy-start.31
  213.1 178.7 %all-reduce.7.cloned.1.call-start = ((), (), s32[]{:S(2)}) async-start(), calls=%async_computation.6 | async-start | bytes 2359296 | tf_op jit(solution)/shard_map/psum | solution.py:269
  221.5 69.9 %copy-start.15 = (bf16[512,3,64]{0,2,1:T(8,128)(2,1)}, bf16[512,3,64]{0,2,1:T(8,128)(2,1)S(1)}, u32[]{:S(2)}) copy-start(bf16[512,3,64]{0,2,1:T(8,128)(2,1)S(1)} %copy.75) | copy-start | bytes 589828
  290.1 1.6 copy-start.9
  291.4 1.0 copy-start.11
  293.2 2.8 copy-start.22
  293.3 2.8 copy-start.38
  293.9 2.1 copy-start.4
  297.8 5.5 %copy-start.16 = (bf16[192,768]{1,0:T(8,128)(2,1)S(1)}, bf16[192,768]{1,0:T(8,128)(2,1)}, u32[]{:S(2)}) copy-start(bf16[192,768]{1,0:T(8,128)(2,1)} %convolution_convert_fusion.3) | copy-start | bytes 884740
  310.8 1.9 copy-start.36
  310.9 115.3 %reduce-scatter.5.cloned.1.call-start = ((), (), s32[]{:S(2)}) async-start(), calls=%async_computation.5 | async-start | bytes 2949120 | tf_op jit(solution)/shard_map/reduce_scatter | solution.py:264
  311.1 1.6 copy-start.40
  313.5 44.2 %copy-start.6 = (bf16[512,768]{1,0:T(8,128)(2,1)S(1)}, bf16[512,768]{1,0:T(8,128)(2,1)}, u32[]{:S(2)}) copy-start(bf16[512,768]{1,0:T(8,128)(2,1)} %get-tuple-element.94) | copy-start | bytes 2359300
  359.3 1.7 copy-start.1
  367.0 61.8 %copy-start.19 = (f32[768]{0:T(1024)}, f32[768]{0:T(1024)S(1)}, u32[]{:S(2)}) copy-start(f32[768]{0:T(1024)S(1)} %get-tuple-element.147) | copy-start | bytes 9220
  396.2 4.4 %copy-start.2 = (bf16[768,768]{1,0:T(8,128)(2,1)S(1)}, bf16[768,768]{1,0:T(8,128)(2,1)}, u32[]{:S(2)}) copy-start(bf16[768,768]{1,0:T(8,128)(2,1)} %all-reduce.7.cloned.1.call-done) | copy-start | bytes 3538948
  401.5 25.9 %copy-start.5 = (f32[512,768]{1,0:T(8,128)S(1)}, f32[512,768]{1,0:T(8,128)}, u32[]{:S(2)}) copy-start(f32[512,768]{1,0:T(8,128)} %get-tuple-element.92) | copy-start | bytes 4718596
  401.5 26.1 %copy-start.8 = (bf16[128,768]{1,0:T(8,128)(2,1)S(1)}, bf16[128,768]{1,0:T(8,128)(2,1)}, u32[]{:S(2)}) copy-start(bf16[128,768]{1,0:T(8,128)(2,1)} %param.29) | copy-start | bytes 589828
  401.5 26.1 %copy-start.14 = (bf16[128,768]{1,0:T(8,128)(2,1)S(1)}, bf16[128,768]{1,0:T(8,128)(2,1)}, u32[]{:S(2)}) copy-start(bf16[128,768]{1,0:T(8,128)(2,1)} %param.15) | copy-start | bytes 589828
  401.5 26.1 %copy-start.32 = (f32[768]{0:T(1024)S(1)}, f32[768]{0:T(1024)}, u32[]{:S(2)}) copy-start(f32[768]{0:T(1024)} %param.28) | copy-start | bytes 9220
  401.5 26.1 %copy-start.33 = (f32[768]{0:T(1024)S(1)}, f32[768]{0:T(1024)}, u32[]{:S(2)}) copy-start(f32[768]{0:T(1024)} %param.24) | copy-start | bytes 9220
Sparse Core Ops, SparseCore 0:
  10.1 22.3 all-gather.5
  41.5 59.9 all-gather.7
  105.7 107.2 all-reduce.4
  216.5 73.5 reduce-scatter.2
  311.0 80.7 all-reduce.6
  394.2 31.9 reduce-scatter.4
